TPU v7x, 32 devices: a whole 2x2x4 slice. The times are simulated.
32 devices in a mesh: seq: 4 (over y, core), fsdp: 8 (over z, x).
Axes of the slice: x: 2, y: 2, z: 4, core: 2. Of those that a mesh axis runs over, the one named last changes fastest.
Arguments:
- latents: bfloat16 [8, 1536, 1536], P('fsdp', 'seq'), may hold values from -48 to 48
- qkv_weight: bfloat16 [1536, 768], P('fsdp'), may hold values from -1 to 1
- out_weight: bfloat16 [256, 1536], P('fsdp'), may hold values from -0.375 to 0.375
- tile_mask: int32 [4, 4], replicated, may hold values from 0 to 1, as said below
- tile_counts: int32 [4], replicated, may hold values from 64 to 384, as said below
Outputs:
- layer_out: bfloat16 [8, 1536, 1536], P('fsdp', 'seq')
Inputs may be any that keep to these rules, and one draw needn't show every extreme that they name: `tile_mask`: tiles are numbered frame first, then 2 along the height, then 2 along the width. Row q marks a box of whole tiles that contains tile q, of at most 4 tiles; row 0 marks exactly 4. `tile_counts`: the real tokens of a tile fill its first slots. Only tiles on the last frame index may be partial; a partial tile holds k * 64 tokens for some k of 1 to 6, the first tile of the last frame index is full, and the last tile is partial with k of 1 to 5.
All inputs are finite; a program needn't handle non-finite values.
Results may differ from a plain program's by a relative error of at most 0.0074.
Values may be sent and summed in bfloat16 or wider, within the bound.
No kernel may reach another device: no remote copies, remote signals or barrier semaphores. Data moves between devices by JAX's collectives and lax.ppermute only.
A program may use at most 64 MiB of HBM per device.

v0:
```python
import jax
import jax.numpy as jnp
from jax import lax
from jax.sharding import PartitionSpec as P

E = 64
TILE = 384
WINDOW = 4


def attend(queries, keys, values, tile_mask, tile_counts):
    tile_total = tile_mask.shape[0]
    score_scale = float(E) ** (-0.5)
    token_live = jnp.arange(TILE, dtype=jnp.int32)[None, :] < tile_counts[:, None]
    query_tiles = queries.reshape(tile_total, TILE, E)
    key_tiles_all = keys.reshape(tile_total, TILE, E)
    value_tiles_all = values.reshape(tile_total, TILE, E)
    tile_numbers = jnp.arange(tile_total, dtype=jnp.int32)

    def one_tile(tile_index):
        mask_row = tile_mask[tile_index]
        tile_order = jnp.argsort((1 - mask_row) * tile_total + tile_numbers)
        key_tiles = tile_order[:WINDOW]
        slot_live = jnp.arange(WINDOW, dtype=jnp.int32) < jnp.sum(mask_row)
        keys_sel = key_tiles_all[key_tiles].reshape(WINDOW * TILE, E)
        values_sel = value_tiles_all[key_tiles].reshape(WINDOW * TILE, E)
        allowed = (token_live[key_tiles] & slot_live[:, None]).reshape(WINDOW * TILE)[None, :]
        scores = (
            lax.dot_general(
                query_tiles[tile_index],
                keys_sel,
                (((1,), (1,)), ((), ())),
                preferred_element_type=jnp.float32,
            )
            * score_scale
        )
        masked = jnp.where(allowed, scores, -1e30)
        row_max = jnp.max(masked, axis=1, keepdims=True)
        numerators = jnp.where(allowed, jnp.exp(masked - row_max), 0.0)
        denominator = jnp.sum(numerators, axis=1, keepdims=True)
        softmax_top = numerators.astype(jnp.bfloat16)
        summed = jnp.dot(softmax_top, values_sel, preferred_element_type=jnp.float32) / denominator
        return jnp.where(token_live[tile_index][:, None], summed, 0.0).astype(jnp.bfloat16)

    return lax.map(one_tile, tile_numbers).reshape(tile_total * TILE, E)


def local(latents, qkv_weight, out_weight, tile_mask, tile_counts):
    seq_count = lax.axis_size("seq")
    local_rows = latents[0]
    row_count = local_rows.shape[0]
    column_count = qkv_weight.shape[1]
    head_columns = column_count // 3
    device_columns = head_columns // seq_count
    full_qkv = lax.all_gather(qkv_weight, "fsdp", axis=0, tiled=True)
    projected = jnp.dot(local_rows, full_qkv, preferred_element_type=jnp.float32)
    projected = projected.astype(jnp.bfloat16).reshape(row_count, 3, seq_count, device_columns)
    by_heads = lax.all_to_all(projected, "seq", split_axis=2, concat_axis=0, tiled=True)
    head_outputs = attend(
        by_heads[:, 0, 0, 0:E],
        by_heads[:, 1, 0, 0:E],
        by_heads[:, 2, 0, 0:E],
        tile_mask,
        tile_counts,
    )
    attended = head_outputs.reshape(seq_count, row_count, device_columns)
    by_tokens = lax.all_to_all(attended, "seq", split_axis=0, concat_axis=2, tiled=True)[0]
    full_out = lax.all_gather(out_weight, "fsdp", axis=0, tiled=True)
    layer_out = jnp.dot(by_tokens, full_out, preferred_element_type=jnp.float32)
    return layer_out.astype(jnp.bfloat16)[None]


def solution(mesh):
    return jax.shard_map(
        local,
        mesh=mesh,
        in_specs=(P("fsdp", "seq", None), P("fsdp", None), P("fsdp", None), P(), P()),
        out_specs=P("fsdp", "seq", None),
        check_vma=False,
    )
```

profile of v0, /device:TPU:0, one launch (start us, length us, event | category | flops | bytes accessed | tf_op | source)
XLA Modules:
  0.0 196.7 jit_solution(5970017230775210502)
XLA Ops:
  6.5 0.7 all-gather.2.cloned.1.call-update
  7.3 57.1 %all-gather.2.cloned.1.call-done = bf16[1536,768]{1,0:T(8,128)(2,1)} async-done(((bf16[192,768]{1,0:T(8,128)(2,1)}), bf16[1536,768]{1,0:T(8,128)(2,1)}) %all-gather.2.cloned.1.call-update) | async-done | bytes 2359312 | tf_op jit(solution)/shard_map/all_gather | solution.py:55
  64.4 2.7 %convolution_convert_fusion.1 = bf16[384,768]{1,0:T(8,128)(2,1)S(1)} fusion(bf16[1536,768]{1,0:T(8,128)(2,1)} %all-gather.2.cloned.1.call-done, bf16[1,384,1536]{2,1,0:T(8,128)(2,1)S(1)} %copy-done), kind=kOutput, calls=%fused_computation.31 | convolution fusion | flops 906264576 | bytes 4128768 | tf_op jit(solution)/shard_map/dot_general | solution.py:56
  67.1 0.3 copy.11
  67.4 0.9 copy.12
  68.3 3.5 %all-to-all-start = ((bf16[384,3,4,64]{0,3,1,2:T(8,128)(2,1)}), bf16[384,3,4,64]{0,3,1,2:T(8,128)(2,1)S(1)}, u32[]{:S(2)}, u32[]{:S(2)}) async-start(bf16[384,3,4,64]{0,3,1,2:T(8,128)(2,1)} %copy.12), calls=%async_computation | async-start | bytes 1179648 | tf_op jit(solution)/shard_map/all_to_all | solution.py:58
  71.8 0.1 iota_compare_fusion.1
  71.9 9.4 %all-to-all-done = bf16[384,3,4,64]{0,3,1,2:T(8,128)(2,1)S(1)} async-done(((bf16[384,3,4,64]{0,3,1,2:T(8,128)(2,1)}), bf16[384,3,4,64]{0,3,1,2:T(8,128)(2,1)S(1)}, u32[]{:S(2)}, u32[]{:S(2)}) %all-to-all-start) | async-done | bytes 589856 | tf_op jit(solution)/shard_map/all_to_all | solution.py:58
  81.4 0.9 copy.17
  82.3 0.9 copy.18
  83.3 0.9 copy.19
  84.2 0.6 iota.18
  84.8 67.9 %while.11 = (s32[]{:T(128)}, bf16[4,384,64]{1,2,0:T(8,128)(2,1)}, s32[4]{0:T(128)}, pred[4,384]{1,0:T(4,128)(4,1)S(1)}, s32[4,4]{1,0:T(4,128)}, /*index=5*/bf16[...) while((s32[]{:T(128)}, bf16[4,384,64]{1,2,0:T(8,128)(2,1)}, ...), condition=%wide.region_5.6_spmd.clone, body=%wide.region_0.5_spmd.clone.sunk | while | flops 156378912 | bytes 8826411 | solution.py:45
  84.8 1.3 dynamic_slice.38
  87.9 0.7 bitcast_add_fusion.2
  88.6 0.8 sort.19
  89.4 0.6 gather_fusion.2
  90.0 1.3 fusion.47
  91.3 0.6 iota_compare_fusion.3
  92.0 0.1 broadcast_and_fusion.2
  92.1 2.3 %gather_fusion.1 = bf16[4,384,64]{2,1,0:T(8,128)(2,1)} fusion(bf16[4,384,64]{2,1,0:T(8,128)(2,1)} %get-tuple-element.193, s32[1024]{0:T(1024)S(1)} %pad_clamp_fusion.2), kind=kCustom, calls=%fused_computation.1.clone.1 | custom fusion | bytes 393232 | tf_op jit(solution)/shard_map/while/body/eval_jaxpr/gather | solution.py:25
  94.4 1.6 fusion.48
  96.0 1.1 fusion.49
  97.2 2.3 %gather_fusion = bf16[4,384,64]{2,1,0:T(8,128)(2,1)} fusion(bf16[4,384,64]{2,1,0:T(8,128)(2,1)} %get-tuple-element.194, s32[1024]{0:T(1024)S(1)} %pad_clamp_fusion.2), kind=kCustom, calls=%fused_computation.2.clone.1 | custom fusion | bytes 393232 | tf_op jit(solution)/shard_map/while/body/eval_jaxpr/gather | solution.py:26
  99.5 2.2 %fusion.50 = bf16[4,384,64]{1,2,0:T(8,128)(2,1)} fusion(bf16[4,384,64]{1,2,0:T(8,128)(2,1)} %get-tuple-element.177, s32[]{:T(128)} %get-tuple-element.176, bf16[1536,64]{1,0:T(8,128)(2,1)} %bitcast.56, f32[384,1536]{1,0:T(8,128)S(1)} %get-tuple-element.163, f32[384]{0:T(512)S(1)} %get-tuple-element.164, pred[1536]{0:T(1024)(128)(4,1)S(1)} %and.25, ...), kind=kOutput, calls=%fused_computation.16.clone.1 | convolution fusion | flops 77340672 | bytes 2807680 | tf_op jit(solution)/shard_map/while/body/eval_jaxpr/dot_general | solution.py:42
  101.7 1.3 dynamic_slice.38
  104.9 0.7 bitcast_add_fusion.2
  105.6 0.8 sort.19
  106.4 0.6 gather_fusion.2
  107.0 1.3 fusion.47
  108.3 0.6 iota_compare_fusion.3
  109.0 0.1 broadcast_and_fusion.2
  109.1 2.3 %gather_fusion.1 = bf16[4,384,64]{2,1,0:T(8,128)(2,1)} fusion(bf16[4,384,64]{2,1,0:T(8,128)(2,1)} %get-tuple-element.193, s32[1024]{0:T(1024)S(1)} %pad_clamp_fusion.2), kind=kCustom, calls=%fused_computation.1.clone.1 | custom fusion | bytes 393232 | tf_op jit(solution)/shard_map/while/body/eval_jaxpr/gather | solution.py:25
  111.4 1.6 fusion.48
  113.0 1.1 fusion.49
  114.1 2.3 %gather_fusion = bf16[4,384,64]{2,1,0:T(8,128)(2,1)} fusion(bf16[4,384,64]{2,1,0:T(8,128)(2,1)} %get-tuple-element.194, s32[1024]{0:T(1024)S(1)} %pad_clamp_fusion.2), kind=kCustom, calls=%fused_computation.2.clone.1 | custom fusion | bytes 393232 | tf_op jit(solution)/shard_map/while/body/eval_jaxpr/gather | solution.py:26
  116.5 2.2 %fusion.50 = bf16[4,384,64]{1,2,0:T(8,128)(2,1)} fusion(bf16[4,384,64]{1,2,0:T(8,128)(2,1)} %get-tuple-element.177, s32[]{:T(128)} %get-tuple-element.176, bf16[1536,64]{1,0:T(8,128)(2,1)} %bitcast.56, f32[384,1536]{1,0:T(8,128)S(1)} %get-tuple-element.163, f32[384]{0:T(512)S(1)} %get-tuple-element.164, pred[1536]{0:T(1024)(128)(4,1)S(1)} %and.25, ...), kind=kOutput, calls=%fused_computation.16.clone.1 | convolution fusion | flops 77340672 | bytes 2807680 | tf_op jit(solution)/shard_map/while/body/eval_jaxpr/dot_general | solution.py:42
  118.7 1.3 dynamic_slice.38
  121.9 0.7 bitcast_add_fusion.2
  122.6 0.8 sort.19
  123.4 0.6 gather_fusion.2
  124.0 1.3 fusion.47
  125.3 0.6 iota_compare_fusion.3
  126.0 0.1 broadcast_and_fusion.2
  126.1 2.3 %gather_fusion.1 = bf16[4,384,64]{2,1,0:T(8,128)(2,1)} fusion(bf16[4,384,64]{2,1,0:T(8,128)(2,1)} %get-tuple-element.193, s32[1024]{0:T(1024)S(1)} %pad_clamp_fusion.2), kind=kCustom, calls=%fused_computation.1.clone.1 | custom fusion | bytes 393232 | tf_op jit(solution)/shard_map/while/body/eval_jaxpr/gather | solution.py:25
  128.4 1.6 fusion.48
  130.0 1.1 fusion.49
  131.1 2.3 %gather_fusion = bf16[4,384,64]{2,1,0:T(8,128)(2,1)} fusion(bf16[4,384,64]{2,1,0:T(8,128)(2,1)} %get-tuple-element.194, s32[1024]{0:T(1024)S(1)} %pad_clamp_fusion.2), kind=kCustom, calls=%fused_computation.2.clone.1 | custom fusion | bytes 393232 | tf_op jit(solution)/shard_map/while/body/eval_jaxpr/gather | solution.py:26
  133.5 2.2 %fusion.50 = bf16[4,384,64]{1,2,0:T(8,128)(2,1)} fusion(bf16[4,384,64]{1,2,0:T(8,128)(2,1)} %get-tuple-element.177, s32[]{:T(128)} %get-tuple-element.176, bf16[1536,64]{1,0:T(8,128)(2,1)} %bitcast.56, f32[384,1536]{1,0:T(8,128)S(1)} %get-tuple-element.163, f32[384]{0:T(512)S(1)} %get-tuple-element.164, pred[1536]{0:T(1024)(128)(4,1)S(1)} %and.25, ...), kind=kOutput, calls=%fused_computation.16.clone.1 | convolution fusion | flops 77340672 | bytes 2807680 | tf_op jit(solution)/shard_map/while/body/eval_jaxpr/dot_general | solution.py:42
  135.7 1.3 dynamic_slice.38
  138.9 0.7 bitcast_add_fusion.2
  139.6 0.8 sort.19
  140.4 0.6 gather_fusion.2
  141.0 1.3 fusion.47
  142.3 0.6 iota_compare_fusion.3
  143.0 0.1 broadcast_and_fusion.2
  143.0 2.3 %gather_fusion.1 = bf16[4,384,64]{2,1,0:T(8,128)(2,1)} fusion(bf16[4,384,64]{2,1,0:T(8,128)(2,1)} %get-tuple-element.193, s32[1024]{0:T(1024)S(1)} %pad_clamp_fusion.2), kind=kCustom, calls=%fused_computation.1.clone.1 | custom fusion | bytes 393232 | tf_op jit(solution)/shard_map/while/body/eval_jaxpr/gather | solution.py:25
  145.4 1.6 fusion.48
  147.0 1.1 fusion.49
  148.1 2.3 %gather_fusion = bf16[4,384,64]{2,1,0:T(8,128)(2,1)} fusion(bf16[4,384,64]{2,1,0:T(8,128)(2,1)} %get-tuple-element.194, s32[1024]{0:T(1024)S(1)} %pad_clamp_fusion.2), kind=kCustom, calls=%fused_computation.2.clone.1 | custom fusion | bytes 393232 | tf_op jit(solution)/shard_map/while/body/eval_jaxpr/gather | solution.py:26
  150.5 2.2 %fusion.50 = bf16[4,384,64]{1,2,0:T(8,128)(2,1)} fusion(bf16[4,384,64]{1,2,0:T(8,128)(2,1)} %get-tuple-element.177, s32[]{:T(128)} %get-tuple-element.176, bf16[1536,64]{1,0:T(8,128)(2,1)} %bitcast.56, f32[384,1536]{1,0:T(8,128)S(1)} %get-tuple-element.163, f32[384]{0:T(512)S(1)} %get-tuple-element.164, pred[1536]{0:T(1024)(128)(4,1)S(1)} %and.25, ...), kind=kOutput, calls=%fused_computation.16.clone.1 | convolution fusion | flops 77340672 | bytes 2807680 | tf_op jit(solution)/shard_map/while/body/eval_jaxpr/dot_general | solution.py:42
  152.7 3.4 %all-to-all-start.1 = ((bf16[4,384,64]{1,2,0:T(8,128)(2,1)}), bf16[4,384,64]{1,2,0:T(8,128)(2,1)S(1)}, u32[]{:S(2)}, u32[]{:S(2)}) async-start(bf16[4,384,64]{1,2,0:T(8,128)(2,1)} %get-tuple-element.51), calls=%async_computation.1 | async-start | bytes 393216 | tf_op jit(solution)/shard_map/all_to_all | solution.py:67
  156.1 32.3 %all_gather.7 = bf16[256,1536]{1,0:T(8,128)(2,1)S(1)} all-gather(bf16[32,1536]{1,0:T(8,128)(2,1)} %param.9), channel_id=1, replica_groups=mesh['seq'=4,'fsdp'=8] {'fsdp'}, dimensions={0}, use_global_device_ids=true | all-gather | bytes 884736 | tf_op jit(solution)/shard_map/all_gather | solution.py:68
  188.3 1.5 fusion.28
  (29 shorter events, 0.4 us)
Async XLA Ops:
  6.5 57.8 %copy-start = (bf16[1,384,1536]{2,1,0:T(8,128)(2,1)S(1)}, bf16[1,384,1536]{2,1,0:T(8,128)(2,1)}, u32[]{:S(2)}) copy-start(bf16[1,384,1536]{2,1,0:T(8,128)(2,1)} %param.7) | copy-start | bytes 3538948
  6.5 57.8 %all-gather.2.cloned.1.call-start = ((), (), s32[]{:S(2)}) async-start(), calls=%async_computation.2 | async-start | bytes 2654208 | tf_op jit(solution)/shard_map/all_gather | solution.py:55
  67.1 4.7 %copy-start.1 = (s32[4]{0:T(128)S(1)}, s32[4]{0:T(128)}, u32[]{:S(2)}) copy-start(s32[4]{0:T(128)} %param.11) | copy-start | bytes 52
  68.3 13.0 %all-to-all-start = ((bf16[384,3,4,64]{0,3,1,2:T(8,128)(2,1)}), bf16[384,3,4,64]{0,3,1,2:T(8,128)(2,1)S(1)}, u32[]{:S(2)}, u32[]{:S(2)}) async-start(bf16[384,3,4,64]{0,3,1,2:T(8,128)(2,1)} %copy.12), calls=%async_computation | async-start | bytes 1179648 | tf_op jit(solution)/shard_map/all_to_all | solution.py:58
  152.7 35.6 %all-to-all-start.1 = ((bf16[4,384,64]{1,2,0:T(8,128)(2,1)}), bf16[4,384,64]{1,2,0:T(8,128)(2,1)S(1)}, u32[]{:S(2)}, u32[]{:S(2)}) async-start(bf16[4,384,64]{1,2,0:T(8,128)(2,1)} %get-tuple-element.51), calls=%async_computation.1 | async-start | bytes 393216 | tf_op jit(solution)/shard_map/all_to_all | solution.py:67
Sparse Core Ops, SparseCore 0:
  9.5 54.7 all-gather.1
where the time goes:
time: 198 us; the launch traced here: 197 us
  waiting for transfers between devices  67.2 us (34%)
  blocking collectives  32.3 us (16%)
  local copies, waits for them, and re-layouts  30.9 us (16%)
  matrix products  19.6 us (10%)
  other arithmetic  18.7 us (9%)
  between operations  13.5 us (7%)
  loops' own time  7.68 us (4%)
  starting transfers between devices  6.84 us (3%)
    all_gather x1, waiting for transfers between devices, local(): full_qkv = lax.all_gather(qkv_weight, 'fsdp', axis=0, tiled=True)  57.1 us
    all_gather x1, blocking collectives, local(): full_out = lax.all_gather(out_weight, 'fsdp', axis=0, tiled=True)  32.3 us
    all_to_all x1, waiting for transfers between devices, local(): lax.all_to_all(projected, 'seq', split_axis=2, concat_axis=0, tiled=True)  9.42 us
    gather x4, local copies, waits for them, and re-layouts, one_tile(): keys_sel = key_tiles_all[key_tiles].reshape(WINDOW * TILE, E)  9.34 us
    gather x4, local copies, waits for them, and re-layouts, one_tile(): values_sel = value_tiles_all[key_tiles].reshape(WINDOW * TILE, E)  9.34 us
    dot_general x4, matrix products, one_tile(): jnp.dot(softmax_top, values_sel, preferred_element_type=jnp.float32)  8.88 us
    another operation x1, loops' own time, attend(): return lax.map(one_tile, tile_numbers).reshape(tile_total * TILE, E)  7.68 us
    dot_general x4, matrix products, one_tile(): lax.dot_general(query_tiles[tile_index], keys_sel, (((1,), (1,)), ((), ()...  6.5 us
  transfers between devices with their start and end apart: 3, of which 2 were waited for; matrix products, arithmetic and copies ran while one was open for 0% of the time, Pallas kernels for 0%

commit v1 on v0

--- a/solution.py
+++ b/solution.py
@@ -6,6 +6,18 @@
 E = 64
 TILE = 384
 WINDOW = 4
+
+
+def gather_by_bits(array, axis, dim):
+    ways, here, lap = (lax.axis_size(axis), lax.axis_index(axis), array.shape[dim])
+    line, have = (array, 1)
+    while have < ways:
+        line = jnp.concatenate(
+            [line, lax.ppermute(line, axis, [(d, (d - have) % ways) for d in range(ways)])],
+            axis=dim,
+        )
+        have = 2 * have
+    return jnp.roll(line, here * lap, axis=dim)
 
 
 def attend(queries, keys, values, tile_mask, tile_counts):
@@ -65,7 +77,7 @@
     )
     attended = head_outputs.reshape(seq_count, row_count, device_columns)
     by_tokens = lax.all_to_all(attended, "seq", split_axis=0, concat_axis=2, tiled=True)[0]
-    full_out = lax.all_gather(out_weight, "fsdp", axis=0, tiled=True)
+    full_out = gather_by_bits(out_weight, "fsdp", 0)
     layer_out = jnp.dot(by_tokens, full_out, preferred_element_type=jnp.float32)
     return layer_out.astype(jnp.bfloat16)[None]
 

time: 198 us -> 159 us (0.80)
  blocking collectives: 32.3 us -> 0 us
  local copies, waits for them, and re-layouts: 30.9 us -> 19.5 us
  starting transfers between devices: 6.84 us -> 14.6 us
  matrix products: 19.6 us -> 12.5 us
  waiting for transfers between devices: 67.2 us -> 70.3 us
    all_gather x1 -> x0, blocking collectives: 32.3 us -> none  [local(): full_out = lax.all_gather(out_weight, 'fsdp', axis=0, tiled=True)]
    all_gather x1, waiting for transfers between devices: 57.1 us -> 24.9 us  [local(): full_qkv = lax.all_gather(qkv_weight, 'fsdp', axis=0, tiled=True)]
    ppermute x0 -> x3, waiting for transfers between devices: none -> 31.9 us  [gather_by_bits(): lax.ppermute(line, axis, [(d, (d - have) % ways) for d in range(ways)])]
    ppermute x0 -> x3, starting transfers between devices: none -> 7.76 us  [gather_by_bits(): lax.ppermute(line, axis, [(d, (d - have) % ways) for d in range(ways)])]
    gather x4, local copies, waits for them, and re-layouts: 9.34 us -> 2.49 us  [one_tile(): values_sel = value_tiles_all[key_tiles].reshape(WINDOW * TILE, E)]
    gather x4, local copies, waits for them, and re-layouts: 9.34 us -> 2.49 us  [one_tile(): keys_sel = key_tiles_all[key_tiles].reshape(WINDOW * TILE, E)]
    all_to_all x1, waiting for transfers between devices: 0.01 us -> 4.53 us  [local(): lax.all_to_all(attended, 'seq', split_axis=0, concat_axis=2, tiled=True)[0]]
    dot_general x4, matrix products: 6.5 us -> 2.28 us  [one_tile(): lax.dot_general(query_tiles[tile_index], keys_sel, (((1,), (1,)), ((), ()...]
  transfers between devices with their start and end apart: 3 -> 6, of which waited for: 2 -> 6; matrix products, arithmetic and copies ran while one was open for 0% -> 4% of each run, Pallas kernels for 0% -> 0%
where the time goes in v1:
time: 159 us; the launch traced here: 158 us
  waiting for transfers between devices  70.3 us (44%)
  other arithmetic  19.6 us (12%)
  local copies, waits for them, and re-layouts  19.5 us (12%)
  starting transfers between devices  14.6 us (9%)
  between operations  13.5 us (8%)
  matrix products  12.5 us (8%)
  loops' own time  8.42 us (5%)
    ppermute x3, waiting for transfers between devices, gather_by_bits(): lax.ppermute(line, axis, [(d, (d - have) % ways) for d in range(ways)])  31.9 us
    all_gather x1, waiting for transfers between devices, local(): full_qkv = lax.all_gather(qkv_weight, 'fsdp', axis=0, tiled=True)  24.9 us
    another operation x1, loops' own time, attend(): return lax.map(one_tile, tile_numbers).reshape(tile_total * TILE, E)  8.42 us
    all_to_all x1, waiting for transfers between devices, local(): lax.all_to_all(projected, 'seq', split_axis=2, concat_axis=0, tiled=True)  8.18 us
    ppermute x3, starting transfers between devices, gather_by_bits(): lax.ppermute(line, axis, [(d, (d - have) % ways) for d in range(ways)])  7.76 us
    reduce_sum x4, other arithmetic, one_tile(): slot_live = jnp.arange(WINDOW, dtype=jnp.int32) < jnp.sum(mask_row)  5.61 us
    dynamic_slice x4, local copies, waits for them, and re-layouts, attend(): return lax.map(one_tile, tile_numbers).reshape(tile_total * TILE, E)  5.27 us
    dot_general x4, matrix products, one_tile(): jnp.dot(softmax_top, values_sel, preferred_element_type=jnp.float32)  4.85 us
  transfers between devices with their start and end apart: 6, of which 6 were waited for; matrix products, arithmetic and copies ran while one was open for 4% of the time, Pallas kernels for 0%

profile of v1, /device:TPU:0, one launch (start us, length us, event | category | flops | bytes accessed | tf_op | source)
XLA Modules:
  0.0 158.3 jit_solution(17350358727004289466)
XLA Ops:
  6.5 0.7 all-gather.2.cloned.1.call-update
  7.3 6.0 %collective-permute-start = (bf16[32,1536]{1,0:T(8,128)(2,1)}, bf16[32,1536]{1,0:T(8,128)(2,1)S(1)}, u32[]{:S(2)}, u32[]{:S(2)}) collective-permute-start(bf16[32,1536]{1,0:T(8,128)(2,1)} %param.9), channel_id=1, source_target_pairs={{0,7},{1,0},{2,1},{3,2},{4,3},{5,4},{6,5},{7,6},{8,15},{9,8},{10,9... | collective-permute-start | bytes 294920 | tf_op jit(solution)/shard_map/ppermute | solution.py:16
  13.3 0.9 constant_dynamic-update-slice_fusion.7
  14.2 1.6 %collective-permute-done = bf16[32,1536]{1,0:T(8,128)(2,1)S(1)} collective-permute-done((bf16[32,1536]{1,0:T(8,128)(2,1)}, bf16[32,1536]{1,0:T(8,128)(2,1)S(1)}, u32[]{:S(2)}, u32[]{:S(2)}) %collective-permute-start) | collective-permute-done | bytes 98336 | tf_op jit(solution)/shard_map/ppermute | solution.py:16
  15.8 0.9 pad_maximum_fusion.1
  16.7 1.4 collective-permute-start.1
  18.2 0.7 iota_compare_fusion.1
  18.9 3.7 %collective-permute-done.1 = bf16[64,1536]{1,0:T(8,128)(2,1)S(1)} collective-permute-done((bf16[64,1536]{1,0:T(8,128)(2,1)S(1)}, bf16[64,1536]{1,0:T(8,128)(2,1)S(1)}, u32[]{:S(2)}, u32[]{:S(2)}) %collective-permute-start.1) | collective-permute-done | bytes 196640 | tf_op jit(solution)/shard_map/ppermute | solution.py:16
  22.6 0.9 pad_maximum_fusion
  23.8 26.6 %collective-permute-done.2 = bf16[128,1536]{1,0:T(8,128)(2,1)S(1)} collective-permute-done((bf16[128,1536]{1,0:T(8,128)(2,1)S(1)}, bf16[128,1536]{1,0:T(8,128)(2,1)S(1)}, u32[]{:S(2)}, u32[]{:S(2)}) %collective-permute-start.2) | collective-permute-done | bytes 393248 | tf_op jit(solution)/shard_map/ppermute | solution.py:16
  50.5 1.2 copy-done.2
  51.7 24.9 %all-gather.2.cloned.1.call-done = bf16[1536,768]{1,0:T(8,128)(2,1)} async-done(((bf16[192,768]{1,0:T(8,128)(2,1)}), bf16[1536,768]{1,0:T(8,128)(2,1)}) %all-gather.2.cloned.1.call-update) | async-done | bytes 2359312 | tf_op jit(solution)/shard_map/all_gather | solution.py:67
  76.6 2.7 %convolution_convert_fusion.1 = bf16[384,768]{1,0:T(8,128)(2,1)S(1)} fusion(bf16[1536,768]{1,0:T(8,128)(2,1)} %all-gather.2.cloned.1.call-done, bf16[1,384,1536]{2,1,0:T(8,128)(2,1)S(1)} %copy-done), kind=kOutput, calls=%fused_computation.31 | convolution fusion | flops 906264576 | bytes 4128768 | tf_op jit(solution)/shard_map/dot_general | solution.py:68
  79.6 0.9 copy.12
  80.5 3.5 %all-to-all-start = ((bf16[384,3,4,64]{0,3,1,2:T(8,128)(2,1)}), bf16[384,3,4,64]{0,3,1,2:T(8,128)(2,1)S(1)}, u32[]{:S(2)}, u32[]{:S(2)}) async-start(bf16[384,3,4,64]{0,3,1,2:T(8,128)(2,1)} %copy.12), calls=%async_computation | async-start | bytes 1179648 | tf_op jit(solution)/shard_map/all_to_all | solution.py:70
  84.0 0.6 constant_dynamic-update-slice_fusion.2
  84.7 0.7 constant_dynamic-update-slice_fusion.1
  85.3 8.2 %all-to-all-done = bf16[384,3,4,64]{0,3,1,2:T(8,128)(2,1)S(1)} async-done(((bf16[384,3,4,64]{0,3,1,2:T(8,128)(2,1)}), bf16[384,3,4,64]{0,3,1,2:T(8,128)(2,1)S(1)}, u32[]{:S(2)}, u32[]{:S(2)}) %all-to-all-start) | async-done | bytes 589856 | tf_op jit(solution)/shard_map/all_to_all | solution.py:70
  94.9 45.3 %while.11 = (s32[]{:T(128)}, bf16[4,384,64]{1,2,0:T(8,128)(2,1)}, s32[4]{0:T(128)}, pred[4,384]{1,0:T(4,128)(4,1)S(1)}, s32[4,4]{1,0:T(4,128)}, /*index=5*/bf16[...) while((s32[]{:T(128)}, bf16[4,384,64]{1,2,0:T(8,128)(2,1)}, ...), condition=%wide.region_5.6_spmd.clone, body=%wide.region_0.5_spmd.clone.sunk | while | flops 156378912 | bytes 8629303 | solution.py:57
  94.9 1.3 dynamic_slice.45
  98.3 0.7 bitcast_add_fusion.2
  99.0 0.8 sort.19
  99.8 0.6 gather_fusion
  100.4 0.6 gather_fusion.1
  101.1 0.6 gather_fusion.2
  101.6 1.4 fusion.48
  103.0 0.7 iota_compare_fusion.3
  103.8 0.6 fusion.49
  104.4 0.5 fusion.50
  105.0 1.2 fusion.51
  106.2 1.3 dynamic_slice.45
  109.6 0.7 bitcast_add_fusion.2
  110.3 0.8 sort.19
  111.1 0.6 gather_fusion
  111.8 0.6 gather_fusion.1
  112.4 0.6 gather_fusion.2
  113.0 1.4 fusion.48
  114.4 0.7 iota_compare_fusion.3
  115.2 0.6 fusion.49
  116.3 1.2 fusion.51
  117.5 1.3 dynamic_slice.45
  120.9 0.7 bitcast_add_fusion.2
  121.6 0.8 sort.19
  122.4 0.6 gather_fusion
  123.1 0.6 gather_fusion.1
  123.7 0.6 gather_fusion.2
  124.3 1.4 fusion.48
  125.7 0.7 iota_compare_fusion.3
  126.5 0.6 fusion.49
  127.6 1.2 fusion.51
  128.8 1.3 dynamic_slice.45
  132.2 0.7 bitcast_add_fusion.2
  132.9 0.8 sort.19
  133.8 0.6 gather_fusion
  134.4 0.6 gather_fusion.1
  135.0 0.6 gather_fusion.2
  135.6 1.4 fusion.48
  137.0 0.7 iota_compare_fusion.3
  137.8 0.6 fusion.49
  138.9 1.2 fusion.51
  140.1 3.4 %all-to-all-start.1 = ((bf16[4,384,64]{1,2,0:T(8,128)(2,1)}), bf16[4,384,64]{1,2,0:T(8,128)(2,1)S(1)}, u32[]{:S(2)}, u32[]{:S(2)}) async-start(bf16[4,384,64]{1,2,0:T(8,128)(2,1)} %get-tuple-element.51), calls=%async_computation.1 | async-start | bytes 393216 | tf_op jit(solution)/shard_map/all_to_all | solution.py:79
  143.5 0.8 constant_dynamic-update-slice_fusion
  144.3 4.5 %all-to-all-done.1 = bf16[4,384,64]{1,2,0:T(8,128)(2,1)S(1)} async-done(((bf16[4,384,64]{1,2,0:T(8,128)(2,1)}), bf16[4,384,64]{1,2,0:T(8,128)(2,1)S(1)}, u32[]{:S(2)}, u32[]{:S(2)}) %all-to-all-start.1) | async-done | bytes 196640 | tf_op jit(solution)/shard_map/all_to_all | solution.py:79
  148.8 2.6 %fusion.28 = bf16[1,384,1536]{2,1,0:T(8,128)(2,1)} fusion(bf16[384,256]{0,1:T(8,128)(2,1)S(1)} %bitcast.61, bf16[512,1536]{1,0:T(8,128)(2,1)} %constant_dynamic-update-slice_fusion, s32[]{:T(128)S(6)} %select_n.35), kind=kOutput, calls=%fused_computation.30 | convolution fusion | flops 302579712 | bytes 2162692 | tf_op jit(solution)/shard_map/dot_general | solution.py:81
  (46 shorter events, 4.1 us)
Async XLA Ops:
  6.5 70.1 %copy-start = (bf16[1,384,1536]{2,1,0:T(8,128)(2,1)S(1)}, bf16[1,384,1536]{2,1,0:T(8,128)(2,1)}, u32[]{:S(2)}) copy-start(bf16[1,384,1536]{2,1,0:T(8,128)(2,1)} %param.7) | copy-start | bytes 3538948
  6.5 44.0 %copy-start.1 = (bf16[32,1536]{1,0:T(8,128)(2,1)S(1)}, bf16[32,1536]{1,0:T(8,128)(2,1)}, u32[]{:S(2)}) copy-start(bf16[32,1536]{1,0:T(8,128)(2,1)} %param.9) | copy-start | bytes 294916
  6.5 70.0 %all-gather.2.cloned.1.call-start = ((), (), s32[]{:S(2)}) async-start(), calls=%async_computation.2 | async-start | bytes 2654208 | tf_op jit(solution)/shard_map/all_gather | solution.py:67
  7.3 8.6 %collective-permute-start = (bf16[32,1536]{1,0:T(8,128)(2,1)}, bf16[32,1536]{1,0:T(8,128)(2,1)S(1)}, u32[]{:S(2)}, u32[]{:S(2)}) collective-permute-start(bf16[32,1536]{1,0:T(8,128)(2,1)} %param.9), channel_id=1, source_target_pairs={{0,7},{1,0},{2,1},{3,2},{4,3},{5,4},{6,5},{7,6},{8,15},{9,8},{10,9... | collective-permute-start | bytes 294920 | tf_op jit(solution)/shard_map/ppermute | solution.py:16
  16.7 5.8 %collective-permute-start.1 = (bf16[64,1536]{1,0:T(8,128)(2,1)S(1)}, bf16[64,1536]{1,0:T(8,128)(2,1)S(1)}, u32[]{:S(2)}, u32[]{:S(2)}) collective-permute-start(bf16[64,1536]{1,0:T(8,128)(2,1)S(1)} %pad_maximum_fusion.1), channel_id=1, source_target_pairs={{0,6},{1,7},{2,0},{3,1},{4,2},{5,3},{6,4},{7,5},{8,14},{9,15},{10,... | collective-permute-start | bytes 589832 | tf_op jit(solution)/shard_map/ppermute | solution.py:16
  23.5 27.0 %collective-permute-start.2 = (bf16[128,1536]{1,0:T(8,128)(2,1)S(1)}, bf16[128,1536]{1,0:T(8,128)(2,1)S(1)}, u32[]{:S(2)}, u32[]{:S(2)}) collective-permute-start(bf16[128,1536]{1,0:T(8,128)(2,1)S(1)} %pad_maximum_fusion), channel_id=1, source_target_pairs={{0,4},{1,5},{2,6},{3,7},{4,0},{5,1},{6,2},{7,3},{8,12},{9,13},{10,... | collective-permute-start | bytes 1179656 | tf_op jit(solution)/shard_map/ppermute | solution.py:16
  50.5 1.2 copy-start.2
  80.5 13.0 %all-to-all-start = ((bf16[384,3,4,64]{0,3,1,2:T(8,128)(2,1)}), bf16[384,3,4,64]{0,3,1,2:T(8,128)(2,1)S(1)}, u32[]{:S(2)}, u32[]{:S(2)}) async-start(bf16[384,3,4,64]{0,3,1,2:T(8,128)(2,1)} %copy.12), calls=%async_computation | async-start | bytes 1179648 | tf_op jit(solution)/shard_map/all_to_all | solution.py:70
  140.1 8.7 %all-to-all-start.1 = ((bf16[4,384,64]{1,2,0:T(8,128)(2,1)}), bf16[4,384,64]{1,2,0:T(8,128)(2,1)S(1)}, u32[]{:S(2)}, u32[]{:S(2)}) async-start(bf16[4,384,64]{1,2,0:T(8,128)(2,1)} %get-tuple-element.51), calls=%async_computation.1 | async-start | bytes 393216 | tf_op jit(solution)/shard_map/all_to_all | solution.py:79
Sparse Core Ops, SparseCore 0:
  9.5 66.9 all-gather.1
